TPU v7x, 32 devices: a whole 2x2x4 slice. The times are simulated.
32 devices in a mesh: rep: 2 (over x), exp: 16 (over z, y, core).
Axes of the slice: x: 2, y: 2, z: 4, core: 2. Of those that a mesh axis runs over, the one named last changes fastest.
Arguments:
- tokens: bfloat16 [1, 128, 7168], P(None, 'exp', 'rep'), may hold values from -6 to 6
- gate_up: bfloat16 [16, 7168, 2, 2048], P('exp', 'rep'), may hold values from -0.09375 to 0.09375
- w_down: bfloat16 [16, 2048, 7168], P('exp', None, 'rep'), may hold values from -0.125 to 0.125
- routes: int32 [1, 128, 8], P(None, 'exp'), may hold values from 0 to 15, all different within a row; in each aligned block of 8 rows (0 to 7, 8 to 15, ..., all dimensions but the last counted through in order) at most 8 rows name the same one
- gates: float32 [1, 128, 8], P(None, 'exp'), may hold values from 0.05 to 1
Outputs:
- mixed_out: bfloat16 [1, 128, 7168], P(None, 'exp', 'rep')
Inputs may be any that keep to these rules, and one draw needn't show every extreme that they name: `routes`: within one step, the 8 tokens of one index of exp name any expert at most 8 times, a bound that some block reaches.
All inputs are finite; a program needn't handle non-finite values.
Results may differ from a plain program's by a relative error of at most 0.024.
Values may be sent and summed in bfloat16 or wider, within the bound.
A program may use at most 192 MiB of HBM per device.

v0:
```python
import jax
import jax.numpy as jnp
from jax import lax
from jax.sharding import PartitionSpec as P


def silu_glu(summed):
    return (jax.nn.silu(summed[:, 0]) * summed[:, 1]).astype(jnp.bfloat16)


def on_device(tokens, gate_up, w_down, routes, gates):
    steps_all, local_tokens, slab_width = tokens.shape
    top_count = routes.shape[2]
    groups = lax.axis_size("exp")
    experts = gate_up.shape[0] * groups
    capacity = max(2, 2 * local_tokens * top_count // experts)
    hidden_units = w_down.shape[1]
    row_count = groups * capacity
    weights_in = gate_up[0].reshape(slab_width, 2 * hidden_units)
    weights_out = w_down[0]
    labels = jnp.arange(experts * capacity, dtype=jnp.int32)
    expert_range = jnp.arange(experts, dtype=jnp.int32)
    expert_ids = routes[0].reshape(-1)
    onehot = (expert_ids[:, None] == expert_range[None, :]).astype(jnp.int32)
    before = jnp.cumsum(onehot, axis=0) - onehot
    slot_rank = jnp.sum(before * onehot, axis=1)
    target_row = expert_ids * capacity + slot_rank
    target_grid = target_row.reshape(local_tokens, top_count)
    placing = jnp.sum(
        (labels[:, None, None] == target_grid[None, :, :]).astype(jnp.int32), axis=2
    ).astype(jnp.bfloat16)
    outgoing = jnp.dot(placing, tokens[0], preferred_element_type=jnp.float32).astype(jnp.bfloat16)
    outgoing = outgoing.reshape(experts, capacity, slab_width)
    arrived = lax.all_to_all(outgoing, "exp", split_axis=0, concat_axis=0, tiled=True)
    partial_value = jnp.dot(
        arrived.reshape(row_count, slab_width), weights_in, preferred_element_type=jnp.float32
    )
    partial_value = partial_value.reshape(row_count, 2, hidden_units)
    shares = lax.psum_scatter(
        partial_value.astype(jnp.bfloat16), "rep", scatter_dimension=0, tiled=True
    ).astype(jnp.float32)
    hidden = silu_glu(shares)
    produced = jnp.dot(
        lax.all_gather(hidden, "rep", axis=0, tiled=True),
        weights_out,
        preferred_element_type=jnp.float32,
    )
    expert_out = produced.astype(jnp.bfloat16).reshape(groups, capacity, slab_width)
    returned = lax.all_to_all(expert_out, "exp", split_axis=0, concat_axis=0, tiled=True).reshape(
        experts * capacity, slab_width
    )
    picked = returned[target_row].reshape(local_tokens, top_count, slab_width).astype(jnp.float32)
    mixed_out = jnp.sum(gates[0][:, :, None] * picked, axis=1).astype(jnp.bfloat16)
    outputs = [mixed_out]
    return jnp.stack(outputs)


def solution(mesh):
    placed = (
        P(None, "exp", "rep"),
        P("exp", "rep", None, None),
        P("exp", None, "rep"),
        P(None, "exp", None),
        P(None, "exp", None),
    )
    return jax.shard_map(
        on_device, mesh=mesh, in_specs=placed, out_specs=P(None, "exp", "rep"), check_vma=False
    )
```

profile of v0, /device:TPU:0, one launch (start us, length us, event | category | flops | bytes accessed | tf_op | source)
XLA Modules:
  0.0 164.6 jit_solution(8216886220679788009)
XLA Ops:
  6.5 0.0 copy-start
  6.5 0.8 eq.31
  7.3 0.1 fusion.14
  7.4 0.1 reduce_window_sum.11
  7.5 0.2 select_reduce_fusion
  7.7 0.1 reduce_sum.32
  7.7 0.7 broadcast_multiply_fusion
  8.5 0.1 convert_reduce_fusion
  8.5 0.0 copy-done
  8.6 1.4 fusion.5
  9.9 7.4 %all-to-all-start = ((bf16[16,8,3584]{2,1,0:T(8,128)(2,1)}), bf16[16,8,3584]{2,1,0:T(8,128)(2,1)S(1)}, u32[]{:S(2)}, u32[]{:S(2)}) async-start(bf16[16,8,3584]{2,1,0:T(8,128)(2,1)} %fusion.5), calls=%async_computation | async-start | bytes 1835008 | tf_op jit(solution)/shard_map/all_to_all | solution.py:34
  17.4 0.0 reduce-scatter.2.cloned.1.call-start
  17.4 20.1 %copy.8 = bf16[448,8,2,2048]{3,1,2,0:T(8,128)(2,1)} copy(bf16[448,8,2,2048]{3,2,1,0:T(2,128)(2,1)} %bitcast.55) | data formatting | bytes 58720256
  37.5 36.0 %copy.7 = bf16[4096,3584]{1,0:T(8,128)(2,1)} copy(bf16[4096,3584]{0,1:T(8,128)(2,1)} %bitcast.54) | data formatting | bytes 58720256 | tf_op jit(solution)/shard_map/dot_general | solution.py:35
  73.4 0.0 all-to-all-done
  73.5 16.1 %convolution_convert_fusion.1 = bf16[128,2,2048]{2,0,1:T(8,128)(2,1)} fusion(bf16[2,2048,3584]{2,1,0:T(8,128)(2,1)} %bitcast.53, bf16[16,8,3584]{2,1,0:T(8,128)(2,1)S(1)} %all-to-all-done), kind=kOutput, calls=%fused_computation.7 | convolution fusion | flops 3758620672 | bytes 31326208 | tf_op jit(solution)/shard_map/dot_general | solution.py:35
  89.5 0.0 reduce-scatter.2.cloned.1.call-update
  89.5 21.9 %reduce-scatter.2.cloned.1.call-done = bf16[64,2,2048]{2,0,1:T(8,128)(2,1)} async-done(((bf16[128,2,2048]{2,0,1:T(8,128)(2,1)}), bf16[64,2,2048]{2,0,1:T(8,128)(2,1)}) %reduce-scatter.2.cloned.1.call-update) | async-done | bytes 524304 | tf_op jit(solution)/shard_map/reduce_scatter | solution.py:39
  111.4 1.1 convert_element_type.48
  112.5 0.0 copy-start.2
  112.5 0.0 copy-start.1
  112.5 0.1 fusion.12
  112.7 8.6 %all_gather.3 = bf16[128,2048]{1,0:T(8,128)(2,1)S(1)} all-gather(bf16[64,2048]{1,0:T(8,128)(2,1)S(1)} %fusion.12), channel_id=1, replica_groups=mesh['rep'=2,'exp'=16] {'rep'}, dimensions={0}, use_global_device_ids=true | all-gather | bytes 786432 | tf_op jit(solution)/shard_map/all_gather | solution.py:44
  121.3 8.2 %fusion.6 = bf16[16,8,3584]{2,1,0:T(8,128)(2,1)} fusion(bf16[128,2048]{1,0:T(8,128)(2,1)S(1)} %all_gather.3, bf16[1,2048,3584]{2,1,0:T(8,128)(2,1)} %param.7), kind=kOutput, calls=%fused_computation.6 | convolution fusion | flops 1879506944 | bytes 16121856 | tf_op jit(solution)/shard_map/dot_general | solution.py:43
  129.5 5.6 %all-to-all-start.1 = ((bf16[16,8,3584]{2,1,0:T(8,128)(2,1)}), bf16[16,8,3584]{2,1,0:T(8,128)(2,1)S(1)}, u32[]{:S(2)}, u32[]{:S(2)}) async-start(bf16[16,8,3584]{2,1,0:T(8,128)(2,1)} %fusion.6), calls=%async_computation.2 | async-start | bytes 1835008 | tf_op jit(solution)/shard_map/all_to_all | solution.py:49
  135.1 0.1 mul.44
  135.2 20.7 %all-to-all-done.1 = bf16[16,8,3584]{2,1,0:T(8,128)(2,1)S(1)} async-done(((bf16[16,8,3584]{2,1,0:T(8,128)(2,1)}), bf16[16,8,3584]{2,1,0:T(8,128)(2,1)S(1)}, u32[]{:S(2)}, u32[]{:S(2)}) %all-to-all-start.1) | async-done | bytes 917536 | tf_op jit(solution)/shard_map/all_to_all | solution.py:49
  155.9 0.8 gather_fusion
  156.7 0.0 copy-done.2
  156.7 1.0 fusion.9
  157.7 0.0 copy-done.1
  (2 shorter events, 0.0 us)
Async XLA Ops:
  6.5 2.0 %copy-start = (bf16[1,8,3584]{2,1,0:T(8,128)(2,1)S(1)}, bf16[1,8,3584]{2,1,0:T(8,128)(2,1)}, u32[]{:S(2)}) copy-start(bf16[1,8,3584]{2,1,0:T(8,128)(2,1)} %param.5) | copy-start | bytes 172036
  9.9 63.5 %all-to-all-start = ((bf16[16,8,3584]{2,1,0:T(8,128)(2,1)}), bf16[16,8,3584]{2,1,0:T(8,128)(2,1)S(1)}, u32[]{:S(2)}, u32[]{:S(2)}) async-start(bf16[16,8,3584]{2,1,0:T(8,128)(2,1)} %fusion.5), calls=%async_computation | async-start | bytes 1835008 | tf_op jit(solution)/shard_map/all_to_all | solution.py:34
  17.4 94.0 %reduce-scatter.2.cloned.1.call-start = ((), (), s32[]{:S(2)}) async-start(), calls=%async_computation.3 | async-start | bytes 1572864 | tf_op jit(solution)/shard_map/reduce_scatter | solution.py:39
  112.5 44.2 %copy-start.2 = (f32[1,8,8]{2,1,0:T(8,128)S(1)}, f32[1,8,8]{2,1,0:T(8,128)}, u32[]{:S(2)}) copy-start(f32[1,8,8]{2,1,0:T(8,128)} %param.9) | copy-start | bytes 772
  112.5 45.2 %copy-start.1 = (bf16[1,8,3584]{2,1,0:T(8,128)(2,1)S(1)}, bf16[1,8,3584]{2,1,0:T(8,128)(2,1)}, u32[]{:S(2)}) copy-start(bf16[1,8,3584]{2,1,0:T(8,128)(2,1)} %param.5) | copy-start | bytes 172036
  129.5 26.4 %all-to-all-start.1 = ((bf16[16,8,3584]{2,1,0:T(8,128)(2,1)}), bf16[16,8,3584]{2,1,0:T(8,128)(2,1)S(1)}, u32[]{:S(2)}, u32[]{:S(2)}) async-start(bf16[16,8,3584]{2,1,0:T(8,128)(2,1)} %fusion.6), calls=%async_computation.2 | async-start | bytes 1835008 | tf_op jit(solution)/shard_map/all_to_all | solution.py:49
Sparse Core Ops, SparseCore 0:
  89.6 21.6 reduce-scatter.1
where the time goes:
time: 167 us; the launch traced here: 165 us
  local copies, waits for them, and re-layouts  57.8 us (35%)
  waiting for transfers between devices  42.6 us (26%)
  matrix products  25.6 us (15%)
  between operations  13.5 us (8%)
  starting transfers between devices  13.1 us (8%)
  blocking collectives  8.55 us (5%)
  other arithmetic  3.48 us (2%)
    dot_general x1, local copies, waits for them, and re-layouts, on_device(): jnp.dot(arrived.reshape(row_count, slab_width), weights_in, preferred_ele...  36 us
    reduce_scatter x1, waiting for transfers between devices, on_device(): lax.psum_scatter(partial_value.astype(jnp.bfloat16), 'rep', scatter_dimen...  21.9 us
    all_to_all x1, waiting for transfers between devices, on_device(): lax.all_to_all(expert_out, 'exp', split_axis=0, concat_axis=0, tiled=True)  20.7 us
    unnamed x7, local copies, waits for them, and re-layouts  20.1 us
    dot_general x1, matrix products, on_device(): jnp.dot(arrived.reshape(row_count, slab_width), weights_in, preferred_ele...  16.1 us
    all_gather x1, blocking collectives, on_device(): lax.all_gather(hidden, 'rep', axis=0, tiled=True)  8.55 us
    dot_general x1, matrix products, on_device(): jnp.dot(lax.all_gather(hidden, 'rep', axis=0, tiled=True), weights_out, p...  8.19 us
    all_to_all x1, starting transfers between devices, on_device(): lax.all_to_all(outgoing, 'exp', split_axis=0, concat_axis=0, tiled=True)  7.41 us
  transfers between devices with their start and end apart: 3, of which 2 were waited for; matrix products, arithmetic and copies ran while one was open for 34% of the time, Pallas kernels for 0%

commit v1 on v0

--- a/solution.py
+++ b/solution.py
@@ -1,6 +1,10 @@
+import functools
+
 import jax
 import jax.numpy as jnp
 from jax import lax
+from jax.experimental import pallas as pl
+from jax.experimental.pallas import tpu as pltpu
 from jax.sharding import PartitionSpec as P
 
 
@@ -55,6 +59,251 @@
     return jnp.stack(outputs)
 
 
+def fused_kernel(
+    n, chunks, pieces, tok_ref, gu_ref, dn_ref, routes_ref, gates_ref, out_ref,
+    xg, wgu, wdn, x2, pbuf, prec, hid, hfull, cbuf, crec, ybuf, yrec, zbuf, zrec,
+    gu_sem, dn_sem, dz_s, dz_r, dy_s, dy_r, dc_s, dc_r,
+    ps_s, ps_r, hs_s, hs_r, rc_s, rc_r, ry_s, ry_r, rz_s, rz_r,
+):
+    rep = lax.axis_index("rep")
+    me = lax.axis_index("exp")
+    zs = n // 4
+    c, y, z = lax.rem(me, 2), lax.rem(me // 2, 2), me // 4
+    rows, width = tok_ref.shape
+    hidden_units = dn_ref.shape[0]
+    cw, pw = hidden_units // chunks, width // pieces
+    half = n * rows // 2
+    other = 1 - rep
+    core_peer = z * 4 + y * 2 + (1 - c)
+    y_peer = z * 4 + (1 - y) * 2 + c
+
+    def z_peer(d):
+        return lax.rem(z + d, zs) * 4 + y * 2 + c
+
+    def remote(src, dst, send, recv, to):
+        return pltpu.make_async_remote_copy(
+            src_ref=src, dst_ref=dst, send_sem=send, recv_sem=recv,
+            device_id=to, device_id_type=pl.DeviceIdType.MESH,
+        )
+
+    barrier = pltpu.get_barrier_semaphore()
+    peers = [(other, me), (rep, core_peer), (rep, y_peer)] + [(rep, z_peer(d)) for d in range(1, zs)]
+    for peer in peers:
+        pl.semaphore_signal(barrier, inc=1, device_id=peer, device_id_type=pl.DeviceIdType.MESH)
+
+    def gu_copy(j):
+        return pltpu.make_async_copy(
+            gu_ref.at[:, :, pl.ds(pl.multiple_of(j * cw, 128), cw)], wgu.at[j], gu_sem.at[j]
+        )
+
+    def dn_copy(q):
+        cols = pl.ds(q * pw, pw)
+        return pltpu.make_async_copy(dn_ref.at[:, cols], wdn.at[:, cols], dn_sem.at[q])
+
+    for j in range(chunks):
+        gu_copy(j).start()
+    for q in range(pieces):
+        dn_copy(q).start()
+
+    lane = lax.broadcasted_iota(jnp.int32, (rows, 128), 1)
+    weight = jnp.zeros((rows, 128), jnp.float32)
+    for k in range(routes_ref.shape[1]):
+        hit = routes_ref[:, k : k + 1] == lax.rem(lane, n)
+        weight = weight + jnp.where(hit, gates_ref[:, k : k + 1], 0.0)
+    high = weight.astype(jnp.bfloat16).astype(jnp.float32)
+    packed = jnp.where(lane < n, high, jnp.where(lane < 2 * n, weight - high, 0.0))
+    xg[me, :, 0:width] = tok_ref[...]
+    xg[me, :, width : width + 128] = packed.astype(jnp.bfloat16)
+    pl.semaphore_wait(barrier, len(peers))
+
+    def source(d, yy):
+        return lax.rem(z - d + zs, zs) * 4 + yy * 2 + c
+
+    def to_z(d):
+        return remote(xg.at[me], xg.at[me], dz_s.at[d], dz_r.at[d], (rep, z_peer(d)))
+
+    def to_y(d):
+        slot = xg.at[source(d, y)]
+        return remote(slot, slot, dy_s.at[d], dy_r.at[d], (rep, y_peer))
+
+    def to_c(d, far):
+        slot = xg.at[source(d, 1 - y if far else y)]
+        at = d + zs * far
+        return remote(slot, slot, dc_s.at[at], dc_r.at[at], (rep, core_peer))
+
+    for d in range(1, zs):
+        to_z(d).start()
+    to_y(0).start()
+    to_c(0, 0).start()
+    for d in range(1, zs):
+        to_z(d).wait_recv()
+        to_y(d).start()
+        to_c(d, 0).start()
+    for d in range(zs):
+        to_y(d).wait_recv()
+        to_c(d, 1).start()
+    for far in range(2):
+        for d in range(zs):
+            to_c(d, far).wait_recv()
+
+    row_at = lax.broadcasted_iota(jnp.int32, (128, 512), 0)
+    col_at = lax.broadcasted_iota(jnp.int32, (128, 512), 1)
+    target = jnp.where(col_at < 256, 2 * row_at, 256 + 2 * row_at + 1)
+    spread = jnp.where(col_at == target, 1.0, 0.0).astype(jnp.bfloat16)
+
+    @pl.loop(0, width // 128)
+    def _(b):
+        part = xg[:, :, pl.ds(pl.multiple_of(b * 128, 128), 128)].reshape(2 * half, 128)
+        both = jnp.dot(part, spread, preferred_element_type=jnp.float32).astype(jnp.bfloat16)
+        cols = pl.ds(pl.multiple_of(b * 256, 256), 256)
+        for h in range(2):
+            x2[2 * h * half : (2 * h + 1) * half, cols] = both[h * half : (h + 1) * half, :256]
+            x2[(2 * h + 1) * half : (2 * h + 2) * half, cols] = both[h * half : (h + 1) * half, 256:]
+
+    def partial_send(j):
+        return remote(pbuf.at[j, other], prec.at[j], ps_s.at[j], ps_r.at[j], (other, me))
+
+    def hidden_send(j):
+        return remote(hid.at[j, rep], hid.at[j, rep], hs_s.at[j], hs_r.at[j], (other, me))
+
+    def hidden_recv(j):
+        return remote(hid.at[j, other], hid.at[j, other], hs_s.at[j], hs_r.at[j], (other, me))
+
+    def finish(j):
+        partial_send(j).wait_recv()
+        total = pbuf[j, rep].astype(jnp.float32) + prec[j].astype(jnp.float32)
+        hid[j, rep] = (jax.nn.silu(total[:half]) * total[half:]).astype(jnp.bfloat16)
+        hidden_send(j).start()
+
+    lag = 2
+
+    @pl.loop(0, chunks)
+    def _(j):
+        gu_copy(j).wait()
+        weights = wgu[j].reshape(2 * width, cw)
+        acc = jnp.dot(x2[...], weights, preferred_element_type=jnp.float32)
+        pbuf[j] = acc.astype(jnp.bfloat16).reshape(2, 2 * half, cw)
+        partial_send(j).start()
+
+        @pl.when(j >= lag)
+        def _():
+            finish(j - lag)
+
+    for j in range(chunks - lag, chunks):
+        finish(j)
+    for j in range(chunks):
+        hidden_recv(j).wait_recv()
+        hfull[:, j * cw : (j + 1) * cw] = hid[j].reshape(2 * half, cw)
+
+    mark = lax.broadcasted_iota(jnp.int32, (2 * half, 128), 1)
+    pair = xg[:, :, width : width + 128].reshape(2 * half, 128).astype(jnp.float32)
+    scale = jnp.sum(jnp.where(lax.rem(mark, n) == me, pair, 0.0), axis=1, keepdims=True)
+
+    def core_send(q):
+        return remote(cbuf.at[q, 1 - c], crec.at[q], rc_s.at[q], rc_r.at[q], (rep, core_peer))
+
+    def y_send(q):
+        return remote(ybuf.at[q, 1 - y], yrec.at[q], ry_s.at[q], ry_r.at[q], (rep, y_peer))
+
+    def z_send(q, d):
+        return remote(
+            zbuf.at[q, lax.rem(z + d, zs)], zrec.at[q, d], rz_s.at[q, d], rz_r.at[q, d], (rep, z_peer(d))
+        )
+
+    def produce(q):
+        dn_copy(q).wait()
+        made = jnp.dot(hfull[...], wdn[:, q * pw : (q + 1) * pw], preferred_element_type=jnp.float32)
+        mixed = (made.astype(jnp.bfloat16).astype(jnp.float32) * scale).astype(jnp.bfloat16)
+        mixed = mixed.reshape(n, rows, pw)
+        for g in range(n):
+            cbuf[q, g % 2, (g // 2) % 2, g // 4] = mixed[g]
+        core_send(q).start()
+
+    def over_core(q):
+        core_send(q).wait_recv()
+        ybuf[q] = (cbuf[q, c].astype(jnp.float32) + crec[q].astype(jnp.float32)).astype(jnp.bfloat16)
+        y_send(q).start()
+
+    def over_y(q):
+        y_send(q).wait_recv()
+        zbuf[q] = (ybuf[q, y].astype(jnp.float32) + yrec[q].astype(jnp.float32)).astype(jnp.bfloat16)
+        for d in range(1, zs):
+            z_send(q, d).start()
+
+    def over_z(q):
+        total = zbuf[q, z].astype(jnp.float32)
+        for d in range(1, zs):
+            z_send(q, d).wait_recv()
+            total = total + zrec[q, d].astype(jnp.float32)
+        out_ref[:, q * pw : (q + 1) * pw] = total.astype(jnp.bfloat16)
+
+    for step in range(pieces + 3):
+        for late, stage in enumerate((produce, over_core, over_y, over_z)):
+            if 0 <= step - late < pieces:
+                stage(step - late)
+
+    for d in range(1, zs):
+        to_z(d).wait_send()
+    for d in range(zs):
+        to_y(d).wait_send()
+        for far in range(2):
+            to_c(d, far).wait_send()
+    for j in range(chunks):
+        partial_send(j).wait_send()
+        hidden_send(j).wait_send()
+    for q in range(pieces):
+        core_send(q).wait_send()
+        y_send(q).wait_send()
+        for d in range(1, zs):
+            z_send(q, d).wait_send()
+
+
+def fused_on_device(tokens, gate_up, w_down, routes, gates):
+    n = lax.axis_size("exp")
+    _, rows, width = tokens.shape
+    hidden_units = w_down.shape[1]
+    chunks, pieces = hidden_units // 256, 4
+    pw, zs, half = width // pieces, n // 4, n * rows // 2
+    bf16, dma = jnp.bfloat16, pltpu.SemaphoreType.DMA
+    vmem = pl.BlockSpec(memory_space=pltpu.VMEM)
+    anywhere = pl.BlockSpec(memory_space=pl.ANY)
+    mixed_out = pl.pallas_call(
+        functools.partial(fused_kernel, n, chunks, pieces),
+        out_shape=jax.ShapeDtypeStruct((rows, width), bf16),
+        in_specs=[vmem, anywhere, anywhere, vmem, vmem],
+        out_specs=vmem,
+        scratch_shapes=[
+            pltpu.VMEM((n, rows, width + 128), bf16),
+            pltpu.VMEM((chunks, width, 2, 256), bf16),
+            pltpu.VMEM((hidden_units, width), bf16),
+            pltpu.VMEM((4 * half, 2 * width), bf16),
+            pltpu.VMEM((chunks, 2, 2 * half, 256), bf16),
+            pltpu.VMEM((chunks, 2 * half, 256), bf16),
+            pltpu.VMEM((chunks, 2, half, 256), bf16),
+            pltpu.VMEM((2 * half, hidden_units), bf16),
+            pltpu.VMEM((pieces, 2, 2, zs, rows, pw), bf16),
+            pltpu.VMEM((pieces, 2, zs, rows, pw), bf16),
+            pltpu.VMEM((pieces, 2, zs, rows, pw), bf16),
+            pltpu.VMEM((pieces, zs, rows, pw), bf16),
+            pltpu.VMEM((pieces, zs, rows, pw), bf16),
+            pltpu.VMEM((pieces, zs, rows, pw), bf16),
+            dma((chunks,)), dma((pieces,)),
+            dma((zs,)), dma((zs,)), dma((zs,)), dma((zs,)), dma((2 * zs,)), dma((2 * zs,)),
+            dma((chunks,)), dma((chunks,)), dma((chunks,)), dma((chunks,)),
+            dma((pieces,)), dma((pieces,)), dma((pieces,)), dma((pieces,)),
+            dma((pieces, zs)), dma((pieces, zs)),
+        ],
+        compiler_params=pltpu.CompilerParams(
+            collective_id=0, has_side_effects=True, vmem_limit_bytes=67043328
+        ),
+    )(tokens[0], gate_up[0], w_down[0], routes[0], gates[0])
+    return mixed_out[None]
+
+
+def fits(mesh):
+    return mesh.shape["rep"] == 2 and mesh.shape["exp"] % 4 == 0 and mesh.shape["exp"] <= 16
+
+
 def solution(mesh):
     placed = (
         P(None, "exp", "rep"),
@@ -64,5 +313,5 @@
         P(None, "exp", None),
     )
     return jax.shard_map(
-        on_device, mesh=mesh, in_specs=placed, out_specs=P(None, "exp", "rep"), check_vma=False
-    )
+        fused_on_device if fits(mesh) else on_device, mesh=mesh, in_specs=placed, out_specs=P(None, "exp", "rep"), check_vma=False
+    )

time: 167 us -> 62.3 us (0.37); the launches traced: 165 us -> 62 us
  Pallas kernels: 0 us -> 60.6 us
  local copies, waits for them, and re-layouts: 57.8 us -> 1.45 us
  waiting for transfers between devices: 42.6 us -> 0 us
  matrix products: 25.6 us -> 0 us
  between operations: 13.5 us -> 0.01 us
  starting transfers between devices: 13.1 us -> 0 us
  blocking collectives: 8.55 us -> 0 us
  other arithmetic: 3.48 us -> 0 us
    pallas_call x0 -> x1, Pallas kernels: none -> 60.6 us  [fused_on_device(): pl.pallas_call(functools.partial(fused_kernel, n, chunks, pieces), out_sh...]
    dot_general x1 -> x0, local copies, waits for them, and re-layouts: 36 us -> none  [on_device(): jnp.dot(arrived.reshape(row_count, slab_width), weights_in, preferred_ele...]
    dot_general x3 -> x0, matrix products: 25.6 us -> none  [the longest x1 16.1 us: on_device(): jnp.dot(arrived.reshape(row_count, slab_width), weights_in, preferred_ele...]
    reduce_scatter x1 -> x0, waiting for transfers between devices: 21.9 us -> none  [on_device(): lax.psum_scatter(partial_value.astype(jnp.bfloat16), 'rep', scatter_dimen...]
    all_to_all x2 -> x0, waiting for transfers between devices: 20.7 us -> none  [the longest x1 20.7 us: on_device(): lax.all_to_all(expert_out, 'exp', split_axis=0, concat_axis=0, tiled=True)]
    unnamed x7 -> x1, local copies, waits for them, and re-layouts: 20.1 us -> 1.45 us
    all_to_all x2 -> x0, starting transfers between devices: 13.1 us -> none  [the longest x1 7.41 us: on_device(): lax.all_to_all(outgoing, 'exp', split_axis=0, concat_axis=0, tiled=True)]
    all_gather x1 -> x0, blocking collectives: 8.55 us -> none  [on_device(): lax.all_gather(hidden, 'rep', axis=0, tiled=True)]
  transfers between devices with their start and end apart: 3 -> 0, of which waited for: 2 -> 0; matrix products, arithmetic and copies ran while one was open for 34% -> 0% of each run, Pallas kernels for 0% -> 0%
where the time goes in v1:
time: 62.3 us; the launch traced here: 62 us
  Pallas kernels  60.6 us (97%)
  local copies, waits for them, and re-layouts  1.45 us (2%)
    pallas_call x1, Pallas kernels, fused_on_device(): pl.pallas_call(functools.partial(fused_kernel, n, chunks, pieces), out_sh...  60.6 us
    unnamed x1, local copies, waits for them, and re-layouts  1.45 us

profile of v1, /device:TPU:0, one launch (start us, length us, event | category | flops | bytes accessed | tf_op | source)
XLA Modules:
  0.0 62.0 jit_solution(14904469638086704443)
XLA Ops:
  0.0 60.6 %shard_map.55 = bf16[8,3584]{1,0:T(8,128)(2,1)} custom-call(bf16[8,3584]{1,0:T(8,128)(2,1)} %bitcast.9, bf16[3584,2,2048]{2,1,0:T(2,128)(2,1)} %bitcast.6, bf16[2048,3584]{1,0:T(8,128)(2,1)} %bitcast.7, s32[8,8]{1,0:T(8,128)} %bitcast.10, f32[8,8]{1,0:T(8,128)} %bitcast.11), custom_call_target="tpu_custom_call" | custom-call | tf_op jit(solution)/shard_map/pallas_call | solution.py:270
  60.6 1.4 %copy.7 = bf16[1,8,3584]{2,1,0:T(8,128)(2,1)} copy(bf16[1,8,3584]{2,1,0:T(8,128)(2,1)} %bitcast.8) | data formatting | bytes 114688
